TPU v7x, 128 devices: a whole 4x4x4 slice. The times are simulated.
128 devices in a mesh: cfg: 2 (over y_hi), group: 16 (over y_lo, x, core), mp: 4 (over z).
Axes of the slice: x: 4, y: 4 (y_hi: 2, y_lo: 2; y = y_hi * 2 + y_lo), z: 4, core: 2. Of those that a mesh axis runs over, the one named last changes fastest.
Arguments:
- latents: float32 [16384, 64], P(('group', 'mp')), may hold values from -0.6 to 0.6
- text_hidden: bfloat16 [2, 8192, 3072], P('cfg', ('group', 'mp')), may hold values from -6 to 6
- w_img_in: bfloat16 [64, 3072], replicated, may hold values from -0.75 to 0.75
- w_img_qkv: bfloat16 [3072, 4608], P(None, 'mp'), may hold values from -1 to 1
- w_txt_kv: bfloat16 [3072, 3072], P(None, 'mp'), may hold values from -0.109375 to 0.109375
- q_gain: float32 [128], replicated, may hold values from 0.25 to 1.75
- k_gain: float32 [128], replicated, may hold values from 0.25 to 1.75
- w_out: bfloat16 [1536, 3072], replicated, may hold values from -1 to 1
- w_final: bfloat16 [3072, 64], replicated, may hold values from -0.109375 to 0.109375
- mod_img: float32 [8, 3, 3072], replicated, may hold values from -3 to 3
- mod_txt: float32 [8, 2, 3072], replicated, may hold values from -3 to 3
- mod_final: float32 [8, 2, 3072], replicated, may hold values from -3 to 3
- guide: float32 [16], replicated, may hold values from 1.5 to 5
- step_size: float32 [8], replicated, may hold values from 0.02 to 0.3
- img_len: int32 [16], replicated, may hold values from 1 to 1024, as said below
- txt_len: int32 [16], replicated, may hold values from 1 to 512, as said below
- split_flag: int32 [2, 16], replicated, may hold values from 0 to 1, as said below
- tstep: int32 [16], replicated, may hold values from 0 to 7
Outputs:
- velocity: float32 [2, 8192, 64], P('cfg', ('group', 'mp'))
- next_latents: float32 [2, 8192, 64], P('cfg', ('group', 'mp'))
Inputs may be any that keep to these rules, and one draw needn't show every extreme that they name: `img_len`: some group has exactly 1024 live image tokens. `txt_len`: some group has exactly 512 live text tokens. `split_flag`: entries [c, 2j] and [c, 2j + 1] are equal; at least one such pair carries 1 and at least one carries 0.
All inputs are finite; a program needn't handle non-finite values.
Results may differ from a plain program's by a relative error of at most 0.035.
Values may be sent and summed in bfloat16 or wider, within the bound.
A program may use at most 192 MiB of HBM per device.

v0:
```python
import jax
import jax.numpy as jnp
from jax import lax
from jax.sharding import PartitionSpec as P

HD = 128


def partner(value, axis, bit):
    mask = 2**bit
    pairs = [(source, source ^ mask) for source in range(lax.axis_size(axis))]
    return lax.ppermute(value, axis, pairs)


def layer_norm(values):
    center = values - jnp.mean(values, -1, keepdims=True)
    spread = jnp.mean(center * center, -1, keepdims=True)
    return center * lax.rsqrt(spread + 1e-06)


def head_norm(values, gain):
    return values * lax.rsqrt(jnp.mean(values * values, -1, keepdims=True) + 1e-06) * gain


def pick_entry(table, index):
    return lax.dynamic_index_in_dim(table, index, 0, keepdims=False)


def local(
    latents,
    text_hidden,
    w_img_in,
    w_img_qkv,
    w_txt_kv,
    q_gain,
    k_gain,
    w_out,
    w_final,
    mod_img,
    mod_txt,
    mod_final,
    guide,
    step_size,
    img_len,
    txt_len,
    split_flag,
    tstep,
):
    group_index = lax.axis_index("group")
    mp_index = lax.axis_index("mp")
    cfg_index = lax.axis_index("cfg")
    mp_count = lax.axis_size("mp")
    mate_index = jnp.bitwise_xor(group_index, 1)
    step_index = pick_entry(tstep, group_index)
    mod_rows = pick_entry(mod_img, step_index)
    text_rows = pick_entry(mod_txt, step_index)
    final_rows = pick_entry(mod_final, step_index)
    shard_rows = latents.shape[0]
    half_rows = shard_rows // 2
    full_img = shard_rows * mp_count
    full_txt = text_hidden.shape[1] * mp_count
    local_heads = w_img_qkv.shape[1] // (3 * HD)
    x_img = jnp.dot(latents.astype(jnp.bfloat16), w_img_in, preferred_element_type=jnp.float32)
    img_mod = (layer_norm(x_img) * (1.0 + mod_rows[1]) + mod_rows[0]).astype(jnp.bfloat16)
    txt_mod = (
        layer_norm(text_hidden[0].astype(jnp.float32)) * (1.0 + text_rows[1]) + text_rows[0]
    ).astype(jnp.bfloat16)
    img_full, txt_full = (
        lax.all_gather(img_mod, "mp", axis=0, tiled=True),
        lax.all_gather(txt_mod, "mp", axis=0, tiled=True),
    )
    qkv = jnp.dot(img_full, w_img_qkv, preferred_element_type=jnp.float32).reshape(
        full_img, local_heads, 3, HD
    )
    query = head_norm(qkv[:, :, 0], q_gain).astype(jnp.bfloat16)
    key_img = head_norm(qkv[:, :, 1], k_gain).astype(jnp.bfloat16)
    value_img = qkv[:, :, 2].astype(jnp.bfloat16)
    text_kv = jnp.dot(txt_full, w_txt_kv, preferred_element_type=jnp.float32).reshape(
        full_txt, local_heads, 2, HD
    )
    key_txt = head_norm(text_kv[:, :, 0], k_gain).astype(jnp.bfloat16)
    value_txt = text_kv[:, :, 1].astype(jnp.bfloat16)
    key_rows = jnp.concatenate([key_txt, key_img], axis=0)
    value_rows = jnp.concatenate([value_txt, value_img], axis=0)
    mate_keys, mate_values = partner((key_rows, value_rows), "group", 0)
    spots_txt = jnp.arange(full_txt, dtype=jnp.int32)
    spots_img = jnp.arange(full_img, dtype=jnp.int32)

    def live_rows(index):
        return jnp.concatenate(
            [spots_txt < pick_entry(txt_len, index), spots_img < pick_entry(img_len, index)]
        )

    flagged = pick_entry(pick_entry(split_flag, cfg_index), group_index) == 1
    live = jnp.concatenate([live_rows(group_index), live_rows(mate_index) & flagged])
    all_keys = jnp.concatenate([key_rows, mate_keys], axis=0)
    all_values = jnp.concatenate([value_rows, mate_values], axis=0)
    scores = jnp.einsum(
        "qhe,khe->hqk", query, all_keys, preferred_element_type=jnp.float32
    ) * HD ** (-0.5)
    scores = jnp.where(live[None, None, :], scores, -1e30)
    weights = jnp.exp(scores - jnp.max(scores, -1, keepdims=True))
    probs = (weights / jnp.sum(weights, -1, keepdims=True)).astype(jnp.bfloat16)
    mixed = jnp.einsum(
        "hqk,khe->qhe", probs, all_values, preferred_element_type=jnp.float32
    ).astype(jnp.bfloat16)
    mixed = mixed.reshape(full_img, local_heads * HD)
    w_local = lax.dynamic_slice_in_dim(w_out, mp_index * local_heads * HD, local_heads * HD, 0)
    attended = lax.psum_scatter(
        jnp.dot(mixed, w_local, preferred_element_type=jnp.float32),
        "mp",
        scatter_dimension=0,
        tiled=True,
    )
    hidden = x_img + mod_rows[2] * attended
    final = (layer_norm(hidden) * (1.0 + final_rows[1]) + final_rows[0]).astype(jnp.bfloat16)
    own_velocity = jnp.dot(final, w_final, preferred_element_type=jnp.float32)
    scale = pick_entry(guide, group_index)
    other_velocity = partner(own_velocity.astype(jnp.bfloat16), "cfg", 0).astype(own_velocity.dtype)
    is_cond = cfg_index == 0
    cond_part = jnp.where(is_cond, own_velocity, other_velocity)
    uncond_part = jnp.where(is_cond, other_velocity, own_velocity)
    guided_all = uncond_part + scale * (cond_part - uncond_part)
    guided = lax.dynamic_slice_in_dim(guided_all, cfg_index * half_rows, half_rows, 0)
    row_place = (
        mp_index * shard_rows + cfg_index * half_rows + jnp.arange(half_rows, dtype=jnp.int32)
    )
    row_live = row_place < pick_entry(img_len, group_index)
    guided = jnp.where(row_live[:, None], guided, 0.0)
    start_rows = lax.dynamic_slice_in_dim(latents, cfg_index * half_rows, half_rows, 0)
    moved = start_rows - pick_entry(step_size, step_index) * guided
    return (guided[None], moved[None])


def solution(mesh):
    placed = (
        P(("group", "mp"), None),
        P("cfg", ("group", "mp"), None),
        P(),
        P(None, "mp"),
        P(None, "mp"),
        P(),
        P(),
        P(),
        P(),
        P(),
        P(),
        P(),
        P(),
        P(),
        P(),
        P(),
        P(),
        P(),
    )
    return jax.shard_map(
        local,
        mesh=mesh,
        in_specs=placed,
        out_specs=(P("cfg", ("group", "mp"), None), P("cfg", ("group", "mp"), None)),
        check_vma=False,
    )
```

profile of v0, /device:TPU:1, one launch (start us, length us, event | category | flops | bytes accessed | tf_op | source)
XLA Modules:
  0.0 342.4 jit_solution(17559711383967402021)
XLA Ops:
  7.2 1.3 dynamic_slice.51
  9.8 1.3 convert_reduce_fusion
  11.1 1.5 fusion.18
  14.3 2.4 fusion.21
  16.8 1.5 fusion.50
  18.8 1.6 constant_dynamic-slice_fusion
  20.3 1.8 add_convert_fusion.1
  25.1 34.8 %all-gather.3.cloned.1.call-done = bf16[512,3072]{1,0:T(8,128)(2,1)} async-done(((bf16[128,3072]{1,0:T(8,128)(2,1)}), bf16[512,3072]{1,0:T(8,128)(2,1)}) %all-gather.3.cloned.1.call-update) | async-done | bytes 3145744 | tf_op jit(solution)/shard_map/all_gather | solution.py:70
  59.9 7.0 %fusion.53 = f32[512,768]{1,0:T(8,128)} fusion(bf16[512,3072]{1,0:T(8,128)(2,1)} %all-gather.3.cloned.1.call-done, bf16[3072,768]{1,0:T(8,128)(2,1)} %param.22), kind=kOutput, calls=%fused_computation.97 | convolution fusion | flops 2415919104 | bytes 9437184 | tf_op jit(solution)/shard_map/dot_general | solution.py:78
  66.9 2.9 reshape.125
  69.8 2.1 slice.60
  72.5 55.0 %all-gather.5.cloned.1.call-done = bf16[1024,3072]{1,0:T(8,128)(2,1)} async-done(((bf16[256,3072]{1,0:T(8,128)(2,1)}), bf16[1024,3072]{1,0:T(8,128)(2,1)}) %all-gather.5.cloned.1.call-update) | async-done | bytes 6291472 | tf_op jit(solution)/shard_map/all_gather | solution.py:69
  127.5 11.3 %fusion.54 = f32[1024,1152]{0,1:T(8,128)S(1)} fusion(bf16[1024,3072]{1,0:T(8,128)(2,1)} %all-gather.5.cloned.1.call-done, bf16[3072,1152]{1,0:T(8,128)(2,1)} %param.21), kind=kOutput, calls=%fused_computation.98 | convolution fusion | flops 7247757312 | bytes 18087936 | tf_op jit(solution)/shard_map/dot_general | solution.py:72
  138.8 2.1 copy-done.2
  140.9 1.3 slice.61
  142.2 3.0 copy.40
  145.2 1.9 fusion.22
  147.1 1.9 fusion.24
  152.4 1.3 dynamic_slice.57
  154.9 3.1 slice.57
  158.0 2.9 copy.41
  160.9 1.5 fusion.30
  163.3 2.1 pad_maximum_fusion.1
  165.4 1.6 multiply_reduce_fusion.2
  167.0 19.6 %fusion.51 = (f32[3,1024]{1,0:T(4,128)}, f32[3,1024,3072]{2,1,0:T(8,128)}) fusion(pred[3072]{0:T(1024)(128)(4,1)} %pad_add_fusion, bf16[1536,3,128]{2,0,1:T(8,128)(2,1)} %collective-permute-done.1, bf16[1024,3,128]{2,0,1:T(8,128)(2,1)} %copy-done.4, bf16[512,3,128]{2,0,1:T(8,128)(2,1)S(1)} %multiply_convert_fusion.1, f32[1024,3,3,128]{0,3,2,1:T(8,128)} %bitcast.91, ...), kind=kOutput, calls=%fused_computation.95 | convolution fusion | flops 2461928448 | bytes 41709056 | tf_op jit(solution)/shard_map/sub | solution.py:102
  186.6 15.0 %fusion.26 = bf16[3,128,1024]{2,1,0:T(8,128)(2,1)S(1)} fusion(f32[3,1024,3072]{2,1,0:T(8,128)} %get-tuple-element.19, f32[3,1024]{1,0:T(4,128)} %get-tuple-element.18, bf16[1536,3,128]{0,2,1:T(8,128)(2,1)} %collective-permute-done, bf16[1024,3,128]{0,2,1:T(8,128)(2,1)} %copy-done.3, bf16[512,3,128]{0,2,1:T(8,128)(2,1)} %bitcast.93), kind=kOutput, calls=%fused_computation.42 | convolution fusion | flops 2442264576 | bytes 40906752 | tf_op jit(solution)/shard_map/hqk,khe->qhe/dot_general | solution.py:104
  201.7 8.1 %fusion.13 = f32[1024,3072]{1,0:T(8,128)} fusion(bf16[1024,384]{0,1:T(8,128)(2,1)S(1)} %bitcast.94, bf16[1536,3072]{1,0:T(8,128)(2,1)} %param.25, s32[]{:T(128)S(6)} %select_n.66), kind=kOutput, calls=%fused_computation.21 | convolution fusion | flops 2415919104 | bytes 15728644 | tf_op jit(solution)/shard_map/dot_general | solution.py:110
  209.8 1.4 dynamic-slice_add_fusion
  211.2 113.8 %reduce-scatter.2.cloned.1.call-done = f32[256,3072]{1,0:T(8,128)} async-done(((f32[1024,3072]{1,0:T(8,128)}), f32[256,3072]{1,0:T(8,128)}) %reduce-scatter.2.cloned.1.call-update) | async-done | bytes 3145744 | tf_op jit(solution)/shard_map/reduce_scatter | solution.py:109
  325.0 2.3 fusion.47
  329.2 2.8 collective-permute-start.2
  334.0 1.9 subtract_bitcast_fusion
  (64 shorter events, 13.6 us)
Async XLA Ops:
  7.2 9.6 %copy-start = (bf16[64,3072]{1,0:T(8,128)(2,1)S(1)}, bf16[64,3072]{1,0:T(8,128)(2,1)}, u32[]{:S(2)}) copy-start(bf16[64,3072]{1,0:T(8,128)(2,1)} %param.20) | copy-start | bytes 1179652
  7.2 52.7 %all-gather.3.cloned.1.call-start = ((), (), s32[]{:S(2)}) async-start(), calls=%async_computation.1 | async-start | bytes 3932160 | tf_op jit(solution)/shard_map/all_gather | solution.py:70
  16.7 110.7 %all-gather.5.cloned.1.call-start = ((), (), s32[]{:S(2)}) async-start(), calls=%async_computation.2 | async-start | bytes 7864320 | tf_op jit(solution)/shard_map/all_gather | solution.py:69
  20.3 2.1 copy-start.8
  20.3 2.1 copy-start.9
  22.2 302.8 %reduce-scatter.2.cloned.1.call-start = ((), (), s32[]{:S(2)}) async-start(), calls=%async_computation.3 | async-start | bytes 15728640 | tf_op jit(solution)/shard_map/reduce_scatter | solution.py:109
  66.9 5.3 %copy-start.10 = (f32[128]{0:T(128)S(1)}, f32[128]{0:T(128)}, u32[]{:S(2)}) copy-start(f32[128]{0:T(128)} %param.24) | copy-start | bytes 1540
  138.8 2.2 copy-start.2
  149.0 0.9 copy-start.4
  151.0 16.0 %collective-permute-start.1 = (bf16[1536,3,128]{2,0,1:T(8,128)(2,1)}, bf16[1536,3,128]{2,0,1:T(8,128)(2,1)}, u32[]{:S(2)}, u32[]{:S(2)}) collective-permute-start(bf16[1536,3,128]{2,0,1:T(8,128)(2,1)} %pad_maximum_fusion.2), channel_id=1, source_target_pairs={{0,4},{4,0},{8,12},{12,8},{16,20},{20,16},{24,28},{28,24},{32,36},... | collective-permute-start | bytes 3538952 | tf_op jit(solution)/shard_map/ppermute | solution.py:12
  162.4 0.9 copy-start.3
  165.4 21.2 %collective-permute-start = (bf16[1536,3,128]{0,2,1:T(8,128)(2,1)}, bf16[1536,3,128]{0,2,1:T(8,128)(2,1)}, u32[]{:S(2)}, u32[]{:S(2)}) collective-permute-start(bf16[1536,3,128]{0,2,1:T(8,128)(2,1)} %pad_maximum_fusion.1), channel_id=1, source_target_pairs={{0,4},{4,0},{8,12},{12,8},{16,20},{20,16},{24,28},{28,24},{32,36},... | collective-permute-start | bytes 3538952 | tf_op jit(solution)/shard_map/ppermute | solution.py:12
  209.8 115.3 %copy-start.6 = (f32[1,1,3072]{2,0,1:T(1,128)S(1)}, f32[1,1,3072]{2,0,1:T(1,128)}, u32[]{:S(2)}) copy-start(f32[1,1,3072]{2,0,1:T(1,128)} %get-tuple-element.4) | copy-start | bytes 36868
  327.4 0.7 copy-start.7
  327.4 1.1 copy-start.11
  327.4 8.5 %copy-start.1 = (bf16[64,3072]{1,0:T(8,128)(2,1)S(1)}, bf16[64,3072]{1,0:T(8,128)(2,1)}, u32[]{:S(2)}) copy-start(bf16[64,3072]{1,0:T(8,128)(2,1)} %param.20) | copy-start | bytes 1179652
  327.4 5.3 %copy-start.12 = (f32[8]{0:T(128)S(1)}, f32[8]{0:T(128)}, u32[]{:S(2)}) copy-start(f32[8]{0:T(128)} %param.31) | copy-start | bytes 100
  327.4 6.0 %copy-start.13 = (f32[16]{0:T(128)S(1)}, f32[16]{0:T(128)}, u32[]{:S(2)}) copy-start(f32[16]{0:T(128)} %param.30) | copy-start | bytes 196
  327.4 6.6 %copy-start.5 = (f32[256,64]{0,1:T(8,128)S(1)}, f32[256,64]{0,1:T(8,128)}, u32[]{:S(2)}) copy-start(f32[256,64]{0,1:T(8,128)} %param.18) | copy-start | bytes 196612
  329.2 4.8 %collective-permute-start.2 = (bf16[256,64]{0,1:T(8,128)(2,1)S(1)}, bf16[256,64]{0,1:T(8,128)(2,1)S(1)}, u32[]{:S(2)}, u32[]{:S(2)}) collective-permute-start(bf16[256,64]{0,1:T(8,128)(2,1)S(1)} %get-tuple-element.20), channel_id=1, source_target_pairs={{0,64},{64,0},{1,65},{65,1},{2,66},{66,2},{3,67},{67,3},{4,68},{68... | collective-permute-start | bytes 98312 | tf_op jit(solution)/shard_map/ppermute | solution.py:12
Sparse Core Ops, SparseCore 0:
  16.8 42.9 all-gather.2
  61.5 65.8 all-gather.4
  209.9 115.0 reduce-scatter.1
where the time goes:
time: 343 us; the launch traced here: 342 us
  waiting for transfers between devices  204 us (59%)
  matrix products  63.3 us (18%)
  other arithmetic  27.7 us (8%)
  local copies, waits for them, and re-layouts  27.4 us (8%)
  between operations  16.7 us (5%)
  starting transfers between devices  3.83 us (1%)
    reduce_scatter x1, waiting for transfers between devices, local(): lax.psum_scatter(jnp.dot(mixed, w_local, preferred_element_type=jnp.float...  114 us
    all_gather x1, waiting for transfers between devices, local(): lax.all_gather(img_mod, 'mp', axis=0, tiled=True)  55 us
    all_gather x1, waiting for transfers between devices, local(): lax.all_gather(txt_mod, 'mp', axis=0, tiled=True)  34.8 us
    sub x1, matrix products, local(): weights = jnp.exp(scores - jnp.max(scores, -1, keepdims=True))  19.6 us
    dot_general x1, matrix products, local(): jnp.einsum('hqk,khe->qhe', probs, all_values, preferred_element_type=jnp....  15 us
    dot_general x1, matrix products, local(): jnp.dot(img_full, w_img_qkv, preferred_element_type=jnp.float32)  11.3 us
    unnamed x30, local copies, waits for them, and re-layouts  10.4 us
    dot_general x1, matrix products, local(): jnp.dot(mixed, w_local, preferred_element_type=jnp.float32)  8.09 us
  transfers between devices with their start and end apart: 6, of which 3 were waited for; matrix products, arithmetic and copies ran while one was open for 17% of the time, Pallas kernels for 0%

commit v1 on v0

--- a/solution.py
+++ b/solution.py
@@ -4,6 +4,12 @@
 from jax.sharding import PartitionSpec as P
 
 HD = 128
+
+
+def gather_by_exchange(x, axis, dim):
+    size = lax.axis_size(axis)
+    repeats = [size if d == dim else 1 for d in range(x.ndim)]
+    return lax.all_to_all(jnp.tile(x, repeats), axis, split_axis=dim, concat_axis=dim, tiled=True)
 
 
 def partner(value, axis, bit):
@@ -67,7 +73,7 @@
     ).astype(jnp.bfloat16)
     img_full, txt_full = (
         lax.all_gather(img_mod, "mp", axis=0, tiled=True),
-        lax.all_gather(txt_mod, "mp", axis=0, tiled=True),
+        gather_by_exchange(txt_mod, "mp", 0),
     )
     qkv = jnp.dot(img_full, w_img_qkv, preferred_element_type=jnp.float32).reshape(
         full_img, local_heads, 3, HD

time: 343 us -> 329 us (0.959)
  waiting for transfers between devices: 204 us -> 183 us
  starting transfers between devices: 3.83 us -> 9.21 us
    all_to_all x0 -> x1, waiting for transfers between devices: none -> 56.4 us  [gather_by_exchange(): lax.all_to_all(jnp.tile(x, repeats), axis, split_axis=dim, concat_axis=di...]
    all_gather x1, waiting for transfers between devices: 55 us -> 13.7 us  [local(): lax.all_gather(img_mod, 'mp', axis=0, tiled=True)]
    all_gather x1 -> x0, waiting for transfers between devices: 34.8 us -> none  [local(): lax.all_gather(txt_mod, 'mp', axis=0, tiled=True)]
    dot_general x0 -> x1, local copies, waits for them, and re-layouts: none -> 7 us  [local(): jnp.dot(txt_full, w_txt_kv, preferred_element_type=jnp.float32)]
    all_to_all x0 -> x1, starting transfers between devices: none -> 5.85 us  [gather_by_exchange(): lax.all_to_all(jnp.tile(x, repeats), axis, split_axis=dim, concat_axis=di...]
    slice x2 -> x0, local copies, waits for them, and re-layouts: 5.24 us -> none  [the longest x1 3.13 us: local(): value_txt = text_kv[:, :, 1].astype(jnp.bfloat16)]
    convert_element_type x0 -> x2, local copies, waits for them, and re-layouts: none -> 3.87 us  [local(): value_txt = text_kv[:, :, 1].astype(jnp.bfloat16)]
    unnamed x30 -> x33, local copies, waits for them, and re-layouts: 10.4 us -> 8.42 us
where the time goes in v1:
time: 329 us; the launch traced here: 327 us
  waiting for transfers between devices  183 us (56%)
  matrix products  62.6 us (19%)
  local copies, waits for them, and re-layouts  28.8 us (9%)
  other arithmetic  26.7 us (8%)
  between operations  17 us (5%)
  starting transfers between devices  9.21 us (3%)
    reduce_scatter x1, waiting for transfers between devices, local(): lax.psum_scatter(jnp.dot(mixed, w_local, preferred_element_type=jnp.float...  113 us
    all_to_all x1, waiting for transfers between devices, gather_by_exchange(): lax.all_to_all(jnp.tile(x, repeats), axis, split_axis=dim, concat_axis=di...  56.4 us
    sub x1, matrix products, local(): weights = jnp.exp(scores - jnp.max(scores, -1, keepdims=True))  19.6 us
    dot_general x1, matrix products, local(): jnp.einsum('hqk,khe->qhe', probs, all_values, preferred_element_type=jnp....  15 us
    all_gather x1, waiting for transfers between devices, local(): lax.all_gather(img_mod, 'mp', axis=0, tiled=True)  13.7 us
    dot_general x1, matrix products, local(): jnp.dot(img_full, w_img_qkv, preferred_element_type=jnp.float32)  11.3 us
    unnamed x33, local copies, waits for them, and re-layouts  8.42 us
    dot_general x1, matrix products, local(): jnp.dot(mixed, w_local, preferred_element_type=jnp.float32)  8.09 us
  transfers between devices with their start and end apart: 6, of which 3 were waited for; matrix products, arithmetic and copies ran while one was open for 17% of the time, Pallas kernels for 0%

profile of v1, /device:TPU:1, one launch (start us, length us, event | category | flops | bytes accessed | tf_op | source)
XLA Modules:
  0.0 327.4 jit_solution(13361720315793575944)
XLA Ops:
  7.2 1.3 dynamic_slice.51
  9.8 1.5 fusion.51
  14.4 1.9 add_convert_fusion.1
  16.3 1.3 convert_reduce_fusion
  17.6 1.5 fusion.18
  19.1 1.5 fusion.21
  20.7 2.0 tile.2
  22.7 5.8 %all-to-all-start = ((bf16[4,128,3072]{2,1,0:T(8,128)(2,1)}), bf16[4,128,3072]{2,1,0:T(8,128)(2,1)}, u32[]{:S(2)}, u32[]{:S(2)}) async-start(bf16[4,128,3072]{2,1,0:T(8,128)(2,1)} %tile.2), calls=%async_computation | async-start | bytes 6291456 | tf_op jit(solution)/shard_map/all_to_all | solution.py:12
  28.6 7.0 %copy.38 = bf16[768,3072]{1,0:T(8,128)(2,1)} copy(bf16[768,3072]{0,1:T(8,128)(2,1)} %bitcast.94) | data formatting | bytes 9437184 | tf_op jit(solution)/shard_map/dot_general | solution.py:84
  40.1 56.4 %all-to-all-done = bf16[4,128,3072]{2,1,0:T(8,128)(2,1)} async-done(((bf16[4,128,3072]{2,1,0:T(8,128)(2,1)}), bf16[4,128,3072]{2,1,0:T(8,128)(2,1)}, u32[]{:S(2)}, u32[]{:S(2)}) %all-to-all-start) | async-done | bytes 3145760 | tf_op jit(solution)/shard_map/all_to_all | solution.py:12
  96.5 6.3 %fusion.54 = f32[512,3,2,128]{3,0,2,1:T(8,128)S(1)} fusion(bf16[512,3072,1,1]{1,0,3,2:T(8,128)(2,1)} %bitcast.8, bf16[3,2,128,3072]{3,2,1,0:T(8,128)(2,1)} %bitcast.95), kind=kOutput, calls=%fused_computation.98 | convolution fusion | flops 2415919104 | bytes 9437184 | tf_op jit(solution)/shard_map/dot_general | solution.py:84
  104.2 13.7 %all-gather.2.cloned.1.call-done = bf16[1024,3072]{1,0:T(8,128)(2,1)} async-done(((bf16[256,3072]{1,0:T(8,128)(2,1)}), bf16[1024,3072]{1,0:T(8,128)(2,1)}) %all-gather.2.cloned.1.call-update) | async-done | bytes 6291472 | tf_op jit(solution)/shard_map/all_gather | solution.py:75
  117.9 11.3 %fusion.55 = f32[1024,1152]{0,1:T(8,128)S(1)} fusion(bf16[1024,3072]{1,0:T(8,128)(2,1)} %all-gather.2.cloned.1.call-done, bf16[3072,1152]{1,0:T(8,128)(2,1)} %param.21), kind=kOutput, calls=%fused_computation.99 | convolution fusion | flops 7247757312 | bytes 18087936 | tf_op jit(solution)/shard_map/dot_general | solution.py:78
  129.2 2.1 copy-done.2
  131.3 1.3 slice.61
  132.6 3.0 copy.43
  135.6 1.9 fusion.22
  137.5 1.9 fusion.24
  140.4 1.1 pad_maximum_fusion.2
  141.9 1.9 fusion.31
  143.8 1.9 copy.32
  145.8 1.5 fusion.30
  148.2 2.1 pad_maximum_fusion.1
  150.4 1.6 multiply_reduce_fusion.2
  152.6 19.6 %fusion.52 = (f32[3,1024]{1,0:T(4,128)}, f32[3,1024,3072]{2,1,0:T(8,128)}) fusion(pred[3072]{0:T(1024)(128)(4,1)S(1)} %pad_add_fusion, bf16[1536,3,128]{2,0,1:T(8,128)(2,1)} %collective-permute-done.1, bf16[1024,3,128]{2,0,1:T(8,128)(2,1)} %copy-done.4, bf16[512,3,128]{2,0,1:T(8,128)(2,1)S(1)} %multiply_convert_fusion.1, f32[1024,3,3,128]{0,3,2,1:T(8,128)} %bitcast.99, ...), kind=kOutput, calls=%fused_computation.96 | convolution fusion | flops 2461928448 | bytes 41713152 | tf_op jit(solution)/shard_map/sub | solution.py:108
  172.2 15.0 %fusion.26 = bf16[3,128,1024]{2,1,0:T(8,128)(2,1)S(1)} fusion(f32[3,1024,3072]{2,1,0:T(8,128)} %get-tuple-element.19, f32[3,1024]{1,0:T(4,128)} %get-tuple-element.18, bf16[1536,3,128]{0,2,1:T(8,128)(2,1)} %collective-permute-done, bf16[1024,3,128]{0,2,1:T(8,128)(2,1)} %copy-done.3, bf16[512,3,128]{0,2,1:T(8,128)(2,1)} %copy.32), kind=kOutput, calls=%fused_computation.42 | convolution fusion | flops 2442264576 | bytes 40906752 | tf_op jit(solution)/shard_map/hqk,khe->qhe/dot_general | solution.py:110
  187.2 8.1 %fusion.13 = f32[1024,3072]{1,0:T(8,128)} fusion(bf16[1024,384]{0,1:T(8,128)(2,1)S(1)} %bitcast.100, bf16[1536,3072]{1,0:T(8,128)(2,1)} %param.25, s32[]{:T(128)S(6)} %select_n.66), kind=kOutput, calls=%fused_computation.21 | convolution fusion | flops 2415919104 | bytes 15728644 | tf_op jit(solution)/shard_map/dot_general | solution.py:116
  195.3 1.4 dynamic-slice_add_fusion
  196.8 113.1 %reduce-scatter.2.cloned.1.call-done = f32[256,3072]{1,0:T(8,128)} async-done(((f32[1024,3072]{1,0:T(8,128)}), f32[256,3072]{1,0:T(8,128)}) %reduce-scatter.2.cloned.1.call-update) | async-done | bytes 3145744 | tf_op jit(solution)/shard_map/reduce_scatter | solution.py:115
  309.9 2.3 fusion.48
  314.0 2.8 collective-permute-start.2
  318.8 1.8 subtract_bitcast_fusion
  (67 shorter events, 14.4 us)
Async XLA Ops:
  7.2 2.6 copy-start
  7.2 110.7 %all-gather.2.cloned.1.call-start = ((), (), s32[]{:S(2)}) async-start(), calls=%async_computation.2 | async-start | bytes 7864320 | tf_op jit(solution)/shard_map/all_gather | solution.py:75
  22.7 73.8 %all-to-all-start = ((bf16[4,128,3072]{2,1,0:T(8,128)(2,1)}), bf16[4,128,3072]{2,1,0:T(8,128)(2,1)}, u32[]{:S(2)}, u32[]{:S(2)}) async-start(bf16[4,128,3072]{2,1,0:T(8,128)(2,1)} %tile.2), calls=%async_computation | async-start | bytes 6291456 | tf_op jit(solution)/shard_map/all_to_all | solution.py:12
  28.5 281.3 %reduce-scatter.2.cloned.1.call-start = ((), (), s32[]{:S(2)}) async-start(), calls=%async_computation.3 | async-start | bytes 15728640 | tf_op jit(solution)/shard_map/reduce_scatter | solution.py:115
  28.5 7.0 %copy-start.12 = (s32[2,16]{1,0:T(2,128)S(1)}, s32[2,16]{1,0:T(2,128)}, u32[]{:S(2)}) copy-start(s32[2,16]{1,0:T(2,128)} %param.34) | copy-start | bytes 388
  28.5 8.3 %copy-start.9 = (s32[16]{0:T(128)S(1)}, s32[16]{0:T(128)}, u32[]{:S(2)}) copy-start(s32[16]{0:T(128)} %param.33) | copy-start | bytes 196
  28.5 8.3 %copy-start.10 = (s32[16]{0:T(128)S(1)}, s32[16]{0:T(128)}, u32[]{:S(2)}) copy-start(s32[16]{0:T(128)} %param.32) | copy-start | bytes 196
  96.5 7.4 %copy-start.11 = (f32[128]{0:T(128)S(1)}, f32[128]{0:T(128)}, u32[]{:S(2)}) copy-start(f32[128]{0:T(128)} %param.24) | copy-start | bytes 1540
  102.8 1.1 copy-start.5
  129.2 2.1 copy-start.2
  139.4 0.9 copy-start.4
  141.4 11.1 %collective-permute-start.1 = (bf16[1536,3,128]{2,0,1:T(8,128)(2,1)}, bf16[1536,3,128]{2,0,1:T(8,128)(2,1)}, u32[]{:S(2)}, u32[]{:S(2)}) collective-permute-start(bf16[1536,3,128]{2,0,1:T(8,128)(2,1)} %pad_maximum_fusion.2), channel_id=1, source_target_pairs={{0,4},{4,0},{8,12},{12,8},{16,20},{20,16},{24,28},{28,24},{32,36},... | collective-permute-start | bytes 3538952 | tf_op jit(solution)/shard_map/ppermute | solution.py:18
  147.3 0.9 copy-start.3
  150.3 21.9 %collective-permute-start = (bf16[1536,3,128]{0,2,1:T(8,128)(2,1)}, bf16[1536,3,128]{0,2,1:T(8,128)(2,1)}, u32[]{:S(2)}, u32[]{:S(2)}) collective-permute-start(bf16[1536,3,128]{0,2,1:T(8,128)(2,1)} %pad_maximum_fusion.1), channel_id=1, source_target_pairs={{0,4},{4,0},{8,12},{12,8},{16,20},{20,16},{24,28},{28,24},{32,36},... | collective-permute-start | bytes 3538952 | tf_op jit(solution)/shard_map/ppermute | solution.py:18
  312.2 0.7 copy-start.7
  312.2 0.7 copy-start.8
  312.2 1.1 copy-start.13
  312.2 8.4 %copy-start.1 = (bf16[64,3072]{1,0:T(8,128)(2,1)S(1)}, bf16[64,3072]{1,0:T(8,128)(2,1)}, u32[]{:S(2)}) copy-start(bf16[64,3072]{1,0:T(8,128)(2,1)} %param.20) | copy-start | bytes 1179652
  312.2 5.3 %copy-start.14 = (f32[8]{0:T(128)S(1)}, f32[8]{0:T(128)}, u32[]{:S(2)}) copy-start(f32[8]{0:T(128)} %param.31) | copy-start | bytes 100
  312.3 5.9 %copy-start.15 = (f32[16]{0:T(128)S(1)}, f32[16]{0:T(128)}, u32[]{:S(2)}) copy-start(f32[16]{0:T(128)} %param.30) | copy-start | bytes 196
  312.3 6.5 %copy-start.6 = (f32[256,64]{0,1:T(8,128)S(1)}, f32[256,64]{0,1:T(8,128)}, u32[]{:S(2)}) copy-start(f32[256,64]{0,1:T(8,128)} %param.18) | copy-start | bytes 196612
  314.0 4.7 %collective-permute-start.2 = (bf16[256,64]{0,1:T(8,128)(2,1)S(1)}, bf16[256,64]{0,1:T(8,128)(2,1)S(1)}, u32[]{:S(2)}, u32[]{:S(2)}) collective-permute-start(bf16[256,64]{0,1:T(8,128)(2,1)S(1)} %get-tuple-element.20), channel_id=1, source_target_pairs={{0,64},{64,0},{1,65},{65,1},{2,66},{66,2},{3,67},{67,3},{4,68},{68... | collective-permute-start | bytes 98312 | tf_op jit(solution)/shard_map/ppermute | solution.py:18
Sparse Core Ops, SparseCore 0:
  16.4 101.4 all-gather.1
  195.4 114.3 reduce-scatter.1
